TPU v7x, 32 devices: a whole 2x2x4 slice. The times are simulated.
32 devices in a mesh: scen: 4 (over y, x), opt: 8 (over z, core).
Axes of the slice: x: 2, y: 2, z: 4, core: 2. Of those that a mesh axis runs over, the one named last changes fastest.
Arguments:
- option_coefs: float32 [4096, 1024], P(('opt', 'scen')), may hold values from -0.75 to 0.75
- underlying_of: int32 [4096, 1], P('opt'), may hold values from 0 to 31; in each aligned block of 128 rows (0 to 127, 128 to 255, ...) at most 8 rows name the same one
- log_return_mean: float32 [32, 1024], P(('scen', 'opt')), may hold values from -1 to 1
- log_return_spread: float32 [32, 1024], P(('scen', 'opt')), may hold values from 1e-06 to 0.0001
- cost: float32 [4096], P('opt'), may hold values from -3 to 3
- positions: float32 [4096], P('opt'), may hold values from -1 to 1
- base_loss: float32 [1024], P('scen'), may hold values from -6 to 6
- duals: float32 [1024], P('scen'), may hold values from 0 to 1
- threshold: float32 [1], replicated, may hold values from -2 to 2
Outputs:
- scenario_values: float32 [4096, 1024], P('opt', 'scen')
- new_positions: float32 [4096], P('opt')
- new_duals: float32 [1024], P('scen')
- new_threshold: float32 [1], replicated
Inputs may be any that keep to these rules, and one draw needn't show every extreme that they name: `underlying_of`: in each aligned block of 128 options no underlying is named more than 8 times, a bound that some block reaches; every underlying is named somewhere.
All inputs are finite; a program needn't handle non-finite values.
Results may differ from a plain program's by a relative error of at most 0.0003.
Values sent between devices are 32-bit elements; how exact they have to be, the bound alone decides.
A program may use at most 64 MiB of HBM per device.

v0:
```python
import math
import jax
import jax.numpy as jnp
from jax import lax
from jax.sharding import PartitionSpec as P

ITERS = 2
LOW_END = -4.0
HIGH_END = 4.0
TAIL_LEVEL = 0.9
PRIMAL_STEP = 0.5
THRESH_STEP = 0.05
DUAL_STEP = 0.5


def cosine_terms(drift_rows, variance_rows, term_count):
    frequency = jnp.arange(term_count, dtype=jnp.float32) * (math.pi / (HIGH_END - LOW_END))
    weight = jnp.where(jnp.arange(term_count) == 0, 0.5, 1.0).astype(jnp.float32) * (
        2.0 / (HIGH_END - LOW_END)
    )
    decay = jnp.exp(-0.5 * variance_rows[:, None] * frequency * frequency)
    return weight * decay * jnp.cos(frequency * (drift_rows[:, None] - LOW_END))


def slot_ranks(owners, label_count):
    onehot = (owners[..., None] == jnp.arange(label_count, dtype=jnp.int32)).astype(jnp.int32)
    before = jnp.cumsum(onehot, axis=1) - onehot
    return jnp.sum(before * onehot, axis=-1)


def on_device(
    option_coefs,
    underlying_of,
    log_return_mean,
    log_return_spread,
    cost,
    positions,
    base_loss,
    duals,
    threshold,
):
    outcome_total = lax.axis_size("scen")
    opt_count = lax.axis_size("opt")
    processor_total = outcome_total * opt_count
    my_row = lax.axis_index("scen")
    block_rows = option_coefs.shape[0]
    term_count = option_coefs.shape[1]
    outcome_lines = duals.shape[0]
    total_scen = log_return_mean.shape[1]
    place_limit = max(2, 2 * block_rows // processor_total)
    column_owner = underlying_of[:, 0].reshape(outcome_total, block_rows)
    column_rank = slot_ranks(column_owner, processor_total)
    my_owner = lax.dynamic_index_in_dim(column_owner, my_row, 0, keepdims=False)
    my_rank = lax.dynamic_index_in_dim(column_rank, my_row, 0, keepdims=False)
    outgoing = jnp.zeros((processor_total * place_limit, term_count), jnp.float32)
    outgoing = outgoing.at[my_owner * place_limit + my_rank].set(option_coefs)
    incoming = lax.all_to_all(
        outgoing.reshape(processor_total, place_limit, term_count),
        ("scen", "opt"),
        split_axis=0,
        concat_axis=0,
        tiled=True,
    )
    incoming = incoming.reshape(outcome_total, opt_count, place_limit, term_count)
    contraction = "abmk,sk->bams"
    holding_buffer_dims = (outcome_total, opt_count, outcome_total, place_limit, outcome_lines)

    def contract_cost_tile(cost_tile_number, valued_contracts):
        drift_rows = lax.dynamic_slice_in_dim(
            log_return_mean[0], cost_tile_number * outcome_lines, outcome_lines
        )
        variance_rows = lax.dynamic_slice_in_dim(
            log_return_spread[0], cost_tile_number * outcome_lines, outcome_lines
        )
        cosine_table = cosine_terms(drift_rows, variance_rows, term_count)
        contract_worths = jnp.einsum(
            contraction, incoming, cosine_table, precision=lax.Precision.HIGHEST
        )
        return lax.dynamic_update_index_in_dim(
            valued_contracts, contract_worths, cost_tile_number, 0
        )

    valued_contracts = lax.fori_loop(
        0, outcome_total, contract_cost_tile, jnp.zeros(holding_buffer_dims, jnp.float32)
    )
    arrived = lax.all_to_all(
        valued_contracts.reshape(processor_total, outcome_total, place_limit, outcome_lines),
        ("scen", "opt"),
        split_axis=0,
        concat_axis=0,
        tiled=True,
    )
    flat_index = (
        column_owner * outcome_total + jnp.arange(outcome_total, dtype=jnp.int32)[:, None]
    ) * place_limit + column_rank
    local_tile = jnp.take(
        arrived.reshape(processor_total * outcome_total * place_limit, outcome_lines),
        flat_index.reshape(-1),
        axis=0,
    )
    root_scen = math.sqrt(total_scen)
    root_opt = math.sqrt(opt_count * local_tile.shape[0])
    tail_mass = (1.0 - TAIL_LEVEL) * total_scen
    holding = positions
    weights = duals
    level = threshold[0]
    for iteration in range(ITERS):
        part_gradient = jnp.dot(local_tile, weights, precision=lax.Precision.HIGHEST)
        gradient_sum, dual_mass = lax.psum((part_gradient, jnp.sum(weights)), "scen")
        holding_next = jnp.clip(
            holding - PRIMAL_STEP * (cost - gradient_sum / root_scen), -1.0, 1.0
        )
        level_next = level - THRESH_STEP * (1.0 - dual_mass / tail_mass)
        holding_bar = 2.0 * holding_next - holding
        level_bar = 2.0 * level_next - level
        part_pnl = jnp.dot(holding_bar, local_tile, precision=lax.Precision.HIGHEST)
        pnl = lax.psum(part_pnl, "opt") / root_opt
        weights = jnp.clip(weights + DUAL_STEP * (base_loss - pnl - level_bar), 0.0, 1.0)
        holding = holding_next
        level = level_next
    return (local_tile, holding, weights, level.reshape(1))


def solution(mesh):
    in_specs = (
        P(("opt", "scen"), None),
        P("opt", None),
        P(("scen", "opt"), None),
        P(("scen", "opt"), None),
        P("opt"),
        P("opt"),
        P("scen"),
        P("scen"),
        P(),
    )
    out_specs = (P("opt", "scen"), P("opt"), P("scen"), P())
    return jax.shard_map(
        on_device, mesh=mesh, in_specs=in_specs, out_specs=out_specs, check_vma=False
    )
```

profile of v0, /device:TPU:0, one launch (start us, length us, event | category | flops | bytes accessed | tf_op | source)
XLA Modules:
  0.0 147.9 jit_solution(6425001164244018007)
XLA Ops:
  0.6 0.7 copy-done.1
  2.0 2.6 %scatter_custom_fusion = f32[256,1024]{1,0:T(8,128)} fusion(s32[128]{0:T(128)S(1)} %fusion.15, f32[128,1024]{1,0:T(8,128)} %param.11, f32[]{:T(128)} %constant.174.clone.1), kind=kCustom, calls=%fused_computation.21 | custom fusion | bytes 1049088 | tf_op jit(solution)/shard_map/scatter | solution.py:56
  4.6 7.3 %all-to-all-start = ((f32[32,8,1024]{2,1,0:T(8,128)}), f32[32,8,1024]{2,1,0:T(8,128)S(1)}, u32[]{:S(2)}, u32[]{:S(2)}) async-start(f32[32,8,1024]{2,1,0:T(8,128)} %bitcast.11), calls=%async_computation | async-start | bytes 2097152 | tf_op jit(solution)/shard_map/all_to_all | solution.py:57
  11.9 27.5 %all-to-all-done = f32[32,8,1024]{2,1,0:T(8,128)S(1)} async-done(((f32[32,8,1024]{2,1,0:T(8,128)}), f32[32,8,1024]{2,1,0:T(8,128)S(1)}, u32[]{:S(2)}, u32[]{:S(2)}) %all-to-all-start) | async-done | bytes 1048608 | tf_op jit(solution)/shard_map/all_to_all | solution.py:57
  39.4 24.5 %while.15 = (s32[]{:T(128)}, f32[4,8,4,8,256]{4,3,2,1,0:T(8,128)}, f32[1,1024]{1,0:T(1,128)}, f32[1,1024]{1,0:T(1,128)}, f32[4,8,8,1024]{3,2,1,0:T(8,128)S(1)}, ...) while((s32[]{:T(128)}, f32[4,8,4,8,256]{4,3,2,1,0:T(8,128)}, f32[1,1024]{1,0:T(1,128)}, ...), condition=%wide.region_4.5_spmd, body=%wide.region_3.4_spmd.sunk | while | flops 806621696 | bytes 1858191 | solution.py:83
  39.4 0.7 dynamic-slice_add_fusion.2
  40.1 4.7 %convolution_bitcast_fusion.2 = f32[1,8,4,8,256]{4,3,1,2,0:T(8,128)S(1)} fusion(f32[4,8,8,1024]{3,2,1,0:T(8,128)S(1)} %get-tuple-element.222, f32[256]{0:T(256)S(1)} %bitcast.56, f32[1024]{0:T(1024)S(1)} %get-tuple-element.197, f32[256]{0:T(256)S(1)} %bitcast.57, f32[1024]{0:T(1024)S(1)} %get-tuple-element.199), kind=kOutput, calls=%fused_computation.2.clone.1 | convolution fusion | flops 806617088 | bytes 1320960 | tf_op jit(solution)/shard_map/while/body/eval_jaxpr/abmk,sk->bams/dot_general | solution.py:76
  44.8 0.7 copy_dynamic-update-slice_fusion.2
  45.5 0.7 dynamic-slice_add_fusion.2
  46.2 4.7 %convolution_bitcast_fusion.2 = f32[1,8,4,8,256]{4,3,1,2,0:T(8,128)S(1)} fusion(f32[4,8,8,1024]{3,2,1,0:T(8,128)S(1)} %get-tuple-element.222, f32[256]{0:T(256)S(1)} %bitcast.56, f32[1024]{0:T(1024)S(1)} %get-tuple-element.197, f32[256]{0:T(256)S(1)} %bitcast.57, f32[1024]{0:T(1024)S(1)} %get-tuple-element.199), kind=kOutput, calls=%fused_computation.2.clone.1 | convolution fusion | flops 806617088 | bytes 1320960 | tf_op jit(solution)/shard_map/while/body/eval_jaxpr/abmk,sk->bams/dot_general | solution.py:76
  50.9 0.7 copy_dynamic-update-slice_fusion.2
  51.6 0.7 dynamic-slice_add_fusion.2
  52.3 4.7 %convolution_bitcast_fusion.2 = f32[1,8,4,8,256]{4,3,1,2,0:T(8,128)S(1)} fusion(f32[4,8,8,1024]{3,2,1,0:T(8,128)S(1)} %get-tuple-element.222, f32[256]{0:T(256)S(1)} %bitcast.56, f32[1024]{0:T(1024)S(1)} %get-tuple-element.197, f32[256]{0:T(256)S(1)} %bitcast.57, f32[1024]{0:T(1024)S(1)} %get-tuple-element.199), kind=kOutput, calls=%fused_computation.2.clone.1 | convolution fusion | flops 806617088 | bytes 1320960 | tf_op jit(solution)/shard_map/while/body/eval_jaxpr/abmk,sk->bams/dot_general | solution.py:76
  57.0 0.7 copy_dynamic-update-slice_fusion.2
  57.7 0.7 dynamic-slice_add_fusion.2
  58.5 4.7 %convolution_bitcast_fusion.2 = f32[1,8,4,8,256]{4,3,1,2,0:T(8,128)S(1)} fusion(f32[4,8,8,1024]{3,2,1,0:T(8,128)S(1)} %get-tuple-element.222, f32[256]{0:T(256)S(1)} %bitcast.56, f32[1024]{0:T(1024)S(1)} %get-tuple-element.197, f32[256]{0:T(256)S(1)} %bitcast.57, f32[1024]{0:T(1024)S(1)} %get-tuple-element.199), kind=kOutput, calls=%fused_computation.2.clone.1 | convolution fusion | flops 806617088 | bytes 1320960 | tf_op jit(solution)/shard_map/while/body/eval_jaxpr/abmk,sk->bams/dot_general | solution.py:76
  63.1 0.7 copy_dynamic-update-slice_fusion.2
  63.9 2.8 %all-to-all-start.1 = ((f32[32,4,8,256]{3,2,1,0:T(8,128)}), f32[32,4,8,256]{3,2,1,0:T(8,128)S(1)}, u32[]{:S(2)}, u32[]{:S(2)}) async-start(f32[32,4,8,256]{3,2,1,0:T(8,128)} %bitcast.13), calls=%async_computation.1 | async-start | bytes 2097152 | tf_op jit(solution)/shard_map/all_to_all | solution.py:86
  68.0 26.2 %all-to-all-done.1 = f32[32,4,8,256]{3,2,1,0:T(8,128)S(1)} async-done(((f32[32,4,8,256]{3,2,1,0:T(8,128)}), f32[32,4,8,256]{3,2,1,0:T(8,128)S(1)}, u32[]{:S(2)}, u32[]{:S(2)}) %all-to-all-start.1) | async-done | bytes 1048608 | tf_op jit(solution)/shard_map/all_to_all | solution.py:86
  94.1 1.6 %gather_fusion = f32[512,256]{1,0:T(8,128)S(1)} fusion(f32[1024,256]{1,0:T(8,128)S(1)} %bitcast.54, s32[1024]{0:T(1024)S(1)} %pad_clamp_fusion), kind=kCustom, calls=%fused_computation | custom fusion | bytes 1050624 | tf_op jit(solution)/shard_map/jit(_take)/gather | solution.py:96
  96.4 8.7 %all-reduce.1 = (f32[512]{0:T(512)S(1)}, f32[]{:T(128)}) all-reduce(f32[512]{0:T(512)S(1)} %bitcast.65, f32[]{:T(128)} %reduce_sum.31), channel_id=1, replica_groups=mesh['scen'=4,'opt'=8] {'scen'}, use_global_device_ids=true, to_apply=%region_5.6 | all-reduce | flops 513 | bytes 4104 | tf_op jit(solution)/shard_map/psum | solution.py:109
  105.4 13.6 %psum.43 = f32[256]{0:T(256)S(1)} all-reduce(f32[256]{0:T(256)S(1)} %bitcast.70), channel_id=1, replica_groups=mesh['scen'=4,'opt'=8] {'opt'}, use_global_device_ids=true, to_apply=%region_6.7 | all-reduce | flops 256 | bytes 2048 | tf_op jit(solution)/shard_map/psum | solution.py:117
  121.5 9.6 %all-reduce = (f32[512]{0:T(512)S(1)}, f32[]{:T(128)}) all-reduce(f32[512]{0:T(512)S(1)} %bitcast.64, f32[]{:T(128)} %get-tuple-element.153), channel_id=1, replica_groups=mesh['scen'=4,'opt'=8] {'scen'}, use_global_device_ids=true, to_apply=%region_9.10 | all-reduce | flops 513 | bytes 4104 | tf_op jit(solution)/shard_map/psum | solution.py:109
  132.6 13.6 %psum.46 = f32[256]{0:T(256)S(1)} all-reduce(f32[256]{0:T(256)S(1)} %bitcast.71), channel_id=1, replica_groups=mesh['scen'=4,'opt'=8] {'opt'}, use_global_device_ids=true, to_apply=%region_10.11 | all-reduce | flops 256 | bytes 2048 | tf_op jit(solution)/shard_map/psum | solution.py:117
  (33 shorter events, 5.5 us)
Async XLA Ops:
  0.6 0.7 copy-start.1
  4.6 34.8 %all-to-all-start = ((f32[32,8,1024]{2,1,0:T(8,128)}), f32[32,8,1024]{2,1,0:T(8,128)S(1)}, u32[]{:S(2)}, u32[]{:S(2)}) async-start(f32[32,8,1024]{2,1,0:T(8,128)} %bitcast.11), calls=%async_computation | async-start | bytes 2097152 | tf_op jit(solution)/shard_map/all_to_all | solution.py:57
  63.9 2.8 %copy-start.2 = (f32[256]{0:T(256)S(1)}, f32[256]{0:T(256)}, u32[]{:S(2)}) copy-start(f32[256]{0:T(256)} %param.18) | copy-start | bytes 3076
  63.9 30.3 %all-to-all-start.1 = ((f32[32,4,8,256]{3,2,1,0:T(8,128)}), f32[32,4,8,256]{3,2,1,0:T(8,128)S(1)}, u32[]{:S(2)}, u32[]{:S(2)}) async-start(f32[32,4,8,256]{3,2,1,0:T(8,128)} %bitcast.13), calls=%async_computation.1 | async-start | bytes 2097152 | tf_op jit(solution)/shard_map/all_to_all | solution.py:86
  95.9 36.4 %copy-start = (f32[512,256]{1,0:T(8,128)}, f32[512,256]{1,0:T(8,128)S(1)}, u32[]{:S(2)}) copy-start(f32[512,256]{1,0:T(8,128)S(1)} %broadcast_select_fusion) | copy-start | bytes 1572868
  96.4 8.7 %copy-start.3 = (f32[512]{0:T(512)S(1)}, f32[512]{0:T(512)}, u32[]{:S(2)}) copy-start(f32[512]{0:T(512)} %param.16) | copy-start | bytes 6148
  96.4 8.7 %copy-start.4 = (f32[512]{0:T(512)S(1)}, f32[512]{0:T(512)}, u32[]{:S(2)}) copy-start(f32[512]{0:T(512)} %param.15) | copy-start | bytes 6148
  119.7 0.7 copy-start.5
where the time goes:
time: 148 us
  waiting for transfers between devices  53.6 us (36%)
  blocking collectives  45.5 us (31%)
  matrix products  20.4 us (14%)
  starting transfers between devices  10.1 us (7%)
  local copies, waits for them, and re-layouts  8.42 us (6%)
  other arithmetic  6.02 us (4%)
  between operations  3.86 us (3%)
    all_to_all x1, waiting for transfers between devices, on_device(): lax.all_to_all(outgoing.reshape(processor_total, place_limit, term_count)...  27.5 us
    psum x2, blocking collectives, on_device(): pnl = lax.psum(part_pnl, 'opt') / root_opt  27.3 us
    all_to_all x1, waiting for transfers between devices, on_device(): lax.all_to_all(valued_contracts.reshape(processor_total, outcome_total, p...  26.2 us
    dot_general x4, matrix products, contract_cost_tile(): jnp.einsum(contraction, incoming, cosine_table, precision=lax.Precision.H...  18.8 us
    psum x2, blocking collectives, on_device(): lax.psum((part_gradient, jnp.sum(weights)), 'scen')  18.2 us
    all_to_all x1, starting transfers between devices, on_device(): lax.all_to_all(outgoing.reshape(processor_total, place_limit, term_count)...  7.33 us
  transfers between devices with their start and end apart: 2, of which 2 were waited for; matrix products, arithmetic and copies ran while one was open for 0% of the time, Pallas kernels for 0%

commit v1 on v0

--- a/solution.py
+++ b/solution.py
@@ -114,7 +114,7 @@
         holding_bar = 2.0 * holding_next - holding
         level_bar = 2.0 * level_next - level
         part_pnl = jnp.dot(holding_bar, local_tile, precision=lax.Precision.HIGHEST)
-        pnl = lax.psum(part_pnl, "opt") / root_opt
+        pnl = jnp.sum(lax.all_gather(part_pnl, "opt"), axis=0) / root_opt
         weights = jnp.clip(weights + DUAL_STEP * (base_loss - pnl - level_bar), 0.0, 1.0)
         holding = holding_next
         level = level_next

time: 148 us -> 140 us (0.946)
  blocking collectives: 45.5 us -> 37.1 us
    psum x2 -> x0, blocking collectives: 27.3 us -> none  [on_device(): pnl = lax.psum(part_pnl, 'opt') / root_opt]
    all_gather x0 -> x2, blocking collectives: none -> 19.9 us  [on_device(): pnl = jnp.sum(lax.all_gather(part_pnl, 'opt'), axis=0) / root_opt]
where the time goes in v1:
time: 140 us
  waiting for transfers between devices  53.6 us (38%)
  blocking collectives  37.1 us (26%)
  matrix products  20.4 us (15%)
  starting transfers between devices  10.1 us (7%)
  local copies, waits for them, and re-layouts  8.42 us (6%)
  other arithmetic  6.07 us (4%)
  between operations  3.86 us (3%)
    all_to_all x1, waiting for transfers between devices, on_device(): lax.all_to_all(outgoing.reshape(processor_total, place_limit, term_count)...  27.5 us
    all_to_all x1, waiting for transfers between devices, on_device(): lax.all_to_all(valued_contracts.reshape(processor_total, outcome_total, p...  26.2 us
    all_gather x2, blocking collectives, on_device(): pnl = jnp.sum(lax.all_gather(part_pnl, 'opt'), axis=0) / root_opt  19.9 us
    dot_general x4, matrix products, contract_cost_tile(): jnp.einsum(contraction, incoming, cosine_table, precision=lax.Precision.H...  18.8 us
    psum x2, blocking collectives, on_device(): lax.psum((part_gradient, jnp.sum(weights)), 'scen')  17.2 us
    all_to_all x1, starting transfers between devices, on_device(): lax.all_to_all(outgoing.reshape(processor_total, place_limit, term_count)...  7.33 us
    dynamic_update_slice x4, local copies, waits for them, and re-layouts, contract_cost_tile(): lax.dynamic_update_index_in_dim(valued_contracts, contract_worths, cost_t...  2.92 us
  transfers between devices with their start and end apart: 2, of which 2 were waited for; matrix products, arithmetic and copies ran while one was open for 0% of the time, Pallas kernels for 0%

profile of v1, /device:TPU:0, one launch (start us, length us, event | category | flops | bytes accessed | tf_op | source)
XLA Modules:
  0.0 139.6 jit_solution(1773420543230276039)
XLA Ops:
  0.6 0.7 copy-done.1
  2.0 2.6 %scatter_custom_fusion = f32[256,1024]{1,0:T(8,128)} fusion(s32[128]{0:T(128)S(1)} %fusion.15, f32[128,1024]{1,0:T(8,128)} %param.11, f32[]{:T(128)} %constant.174.clone.1), kind=kCustom, calls=%fused_computation.23 | custom fusion | bytes 1049088 | tf_op jit(solution)/shard_map/scatter | solution.py:56
  4.6 7.3 %all-to-all-start = ((f32[32,8,1024]{2,1,0:T(8,128)}), f32[32,8,1024]{2,1,0:T(8,128)S(1)}, u32[]{:S(2)}, u32[]{:S(2)}) async-start(f32[32,8,1024]{2,1,0:T(8,128)} %bitcast.11), calls=%async_computation | async-start | bytes 2097152 | tf_op jit(solution)/shard_map/all_to_all | solution.py:57
  11.9 27.5 %all-to-all-done = f32[32,8,1024]{2,1,0:T(8,128)S(1)} async-done(((f32[32,8,1024]{2,1,0:T(8,128)}), f32[32,8,1024]{2,1,0:T(8,128)S(1)}, u32[]{:S(2)}, u32[]{:S(2)}) %all-to-all-start) | async-done | bytes 1048608 | tf_op jit(solution)/shard_map/all_to_all | solution.py:57
  39.4 24.5 %while.15 = (s32[]{:T(128)}, f32[4,8,4,8,256]{4,3,2,1,0:T(8,128)}, f32[1,1024]{1,0:T(1,128)}, f32[1,1024]{1,0:T(1,128)}, f32[4,8,8,1024]{3,2,1,0:T(8,128)S(1)}, ...) while((s32[]{:T(128)}, f32[4,8,4,8,256]{4,3,2,1,0:T(8,128)}, f32[1,1024]{1,0:T(1,128)}, ...), condition=%wide.region_4.5_spmd, body=%wide.region_3.4_spmd.sunk | while | flops 806621696 | bytes 1858191 | solution.py:83
  39.4 0.7 dynamic-slice_add_fusion.2
  40.1 4.7 %convolution_bitcast_fusion.4 = f32[1,8,4,8,256]{4,3,1,2,0:T(8,128)S(1)} fusion(f32[4,8,8,1024]{3,2,1,0:T(8,128)S(1)} %get-tuple-element.222, f32[256]{0:T(256)S(1)} %bitcast.62, f32[1024]{0:T(1024)S(1)} %get-tuple-element.197, f32[256]{0:T(256)S(1)} %bitcast.63, f32[1024]{0:T(1024)S(1)} %get-tuple-element.199), kind=kOutput, calls=%fused_computation.2.clone.1 | convolution fusion | flops 806617088 | bytes 1320960 | tf_op jit(solution)/shard_map/while/body/eval_jaxpr/abmk,sk->bams/dot_general | solution.py:76
  44.8 0.7 copy_dynamic-update-slice_fusion.2
  45.5 0.7 dynamic-slice_add_fusion.2
  46.2 4.7 %convolution_bitcast_fusion.4 = f32[1,8,4,8,256]{4,3,1,2,0:T(8,128)S(1)} fusion(f32[4,8,8,1024]{3,2,1,0:T(8,128)S(1)} %get-tuple-element.222, f32[256]{0:T(256)S(1)} %bitcast.62, f32[1024]{0:T(1024)S(1)} %get-tuple-element.197, f32[256]{0:T(256)S(1)} %bitcast.63, f32[1024]{0:T(1024)S(1)} %get-tuple-element.199), kind=kOutput, calls=%fused_computation.2.clone.1 | convolution fusion | flops 806617088 | bytes 1320960 | tf_op jit(solution)/shard_map/while/body/eval_jaxpr/abmk,sk->bams/dot_general | solution.py:76
  50.9 0.7 copy_dynamic-update-slice_fusion.2
  51.6 0.7 dynamic-slice_add_fusion.2
  52.3 4.7 %convolution_bitcast_fusion.4 = f32[1,8,4,8,256]{4,3,1,2,0:T(8,128)S(1)} fusion(f32[4,8,8,1024]{3,2,1,0:T(8,128)S(1)} %get-tuple-element.222, f32[256]{0:T(256)S(1)} %bitcast.62, f32[1024]{0:T(1024)S(1)} %get-tuple-element.197, f32[256]{0:T(256)S(1)} %bitcast.63, f32[1024]{0:T(1024)S(1)} %get-tuple-element.199), kind=kOutput, calls=%fused_computation.2.clone.1 | convolution fusion | flops 806617088 | bytes 1320960 | tf_op jit(solution)/shard_map/while/body/eval_jaxpr/abmk,sk->bams/dot_general | solution.py:76
  57.0 0.7 copy_dynamic-update-slice_fusion.2
  57.7 0.7 dynamic-slice_add_fusion.2
  58.5 4.7 %convolution_bitcast_fusion.4 = f32[1,8,4,8,256]{4,3,1,2,0:T(8,128)S(1)} fusion(f32[4,8,8,1024]{3,2,1,0:T(8,128)S(1)} %get-tuple-element.222, f32[256]{0:T(256)S(1)} %bitcast.62, f32[1024]{0:T(1024)S(1)} %get-tuple-element.197, f32[256]{0:T(256)S(1)} %bitcast.63, f32[1024]{0:T(1024)S(1)} %get-tuple-element.199), kind=kOutput, calls=%fused_computation.2.clone.1 | convolution fusion | flops 806617088 | bytes 1320960 | tf_op jit(solution)/shard_map/while/body/eval_jaxpr/abmk,sk->bams/dot_general | solution.py:76
  63.1 0.7 copy_dynamic-update-slice_fusion.2
  63.9 2.8 %all-to-all-start.1 = ((f32[32,4,8,256]{3,2,1,0:T(8,128)}), f32[32,4,8,256]{3,2,1,0:T(8,128)S(1)}, u32[]{:S(2)}, u32[]{:S(2)}) async-start(f32[32,4,8,256]{3,2,1,0:T(8,128)} %bitcast.13), calls=%async_computation.1 | async-start | bytes 2097152 | tf_op jit(solution)/shard_map/all_to_all | solution.py:86
  68.0 26.2 %all-to-all-done.1 = f32[32,4,8,256]{3,2,1,0:T(8,128)S(1)} async-done(((f32[32,4,8,256]{3,2,1,0:T(8,128)}), f32[32,4,8,256]{3,2,1,0:T(8,128)S(1)}, u32[]{:S(2)}, u32[]{:S(2)}) %all-to-all-start.1) | async-done | bytes 1048608 | tf_op jit(solution)/shard_map/all_to_all | solution.py:86
  94.1 1.6 %gather_fusion = f32[512,256]{1,0:T(8,128)S(1)} fusion(f32[1024,256]{1,0:T(8,128)S(1)} %bitcast.60, s32[1024]{0:T(1024)S(1)} %pad_clamp_fusion), kind=kCustom, calls=%fused_computation | custom fusion | bytes 1050624 | tf_op jit(solution)/shard_map/jit(_take)/gather | solution.py:96
  96.4 8.7 %all-reduce.1 = (f32[512]{0:T(512)S(1)}, f32[]{:T(128)}) all-reduce(f32[512]{0:T(512)S(1)} %bitcast.71, f32[]{:T(128)} %reduce_sum.50), channel_id=1, replica_groups=mesh['scen'=4,'opt'=8] {'scen'}, use_global_device_ids=true, to_apply=%region_5.6 | all-reduce | flops 513 | bytes 4104 | tf_op jit(solution)/shard_map/psum | solution.py:109
  105.4 10.3 %all-gather.2 = f32[8,1,256]{2,1,0:T(1,128)S(1)} all-gather(f32[1,1,256]{2,1,0:T(1,128)S(1)} %convolution_bitcast_fusion.2), channel_id=2, replica_groups=mesh['scen'=4,'opt'=8] {'opt'}, dimensions={0}, use_global_device_ids=true | all-gather | bytes 9216 | tf_op jit(solution)/shard_map/all_gather | solution.py:117
  118.2 8.6 %all-reduce = (f32[512]{0:T(512)S(1)}, f32[]{:T(128)}) all-reduce(f32[512]{0:T(512)S(1)} %bitcast.70, f32[]{:T(128)} %get-tuple-element.153), channel_id=1, replica_groups=mesh['scen'=4,'opt'=8] {'scen'}, use_global_device_ids=true, to_apply=%region_9.10 | all-reduce | flops 513 | bytes 4104 | tf_op jit(solution)/shard_map/psum | solution.py:109
  128.3 9.6 %all-gather.3 = f32[8,1,256]{2,1,0:T(1,128)S(1)} all-gather(f32[1,1,256]{2,1,0:T(1,128)S(1)} %convolution_bitcast_fusion.1), channel_id=3, replica_groups=mesh['scen'=4,'opt'=8] {'opt'}, dimensions={0}, use_global_device_ids=true | all-gather | bytes 9216 | tf_op jit(solution)/shard_map/all_gather | solution.py:117
  (35 shorter events, 5.6 us)
Async XLA Ops:
  0.6 0.7 copy-start.1
  4.6 34.8 %all-to-all-start = ((f32[32,8,1024]{2,1,0:T(8,128)}), f32[32,8,1024]{2,1,0:T(8,128)S(1)}, u32[]{:S(2)}, u32[]{:S(2)}) async-start(f32[32,8,1024]{2,1,0:T(8,128)} %bitcast.11), calls=%async_computation | async-start | bytes 2097152 | tf_op jit(solution)/shard_map/all_to_all | solution.py:57
  63.9 2.8 %copy-start.2 = (f32[256]{0:T(256)S(1)}, f32[256]{0:T(256)}, u32[]{:S(2)}) copy-start(f32[256]{0:T(256)} %param.18) | copy-start | bytes 3076
  63.9 30.3 %all-to-all-start.1 = ((f32[32,4,8,256]{3,2,1,0:T(8,128)}), f32[32,4,8,256]{3,2,1,0:T(8,128)S(1)}, u32[]{:S(2)}, u32[]{:S(2)}) async-start(f32[32,4,8,256]{3,2,1,0:T(8,128)} %bitcast.13), calls=%async_computation.1 | async-start | bytes 2097152 | tf_op jit(solution)/shard_map/all_to_all | solution.py:86
  95.9 32.2 %copy-start = (f32[512,256]{1,0:T(8,128)}, f32[512,256]{1,0:T(8,128)S(1)}, u32[]{:S(2)}) copy-start(f32[512,256]{1,0:T(8,128)S(1)} %broadcast_select_fusion) | copy-start | bytes 1572868
  96.4 8.7 %copy-start.3 = (f32[512]{0:T(512)S(1)}, f32[512]{0:T(512)}, u32[]{:S(2)}) copy-start(f32[512]{0:T(512)} %param.16) | copy-start | bytes 6148
  96.4 8.7 %copy-start.4 = (f32[512]{0:T(512)S(1)}, f32[512]{0:T(512)}, u32[]{:S(2)}) copy-start(f32[512]{0:T(512)} %param.15) | copy-start | bytes 6148
  116.4 0.7 copy-start.5
